TPU v7x, 256 devices: a whole 4x4x8 slice. The times are simulated.
256 devices in a mesh: seq: 8 (over x, core), exp: 32 (over y, z).
Axes of the slice: x: 4, y: 4, z: 8, core: 2. Of those that a mesh axis runs over, the one named last changes fastest.
Arguments:
- tokens: bfloat16 [4096, 7168], P('exp', 'seq'), may hold values from -6 to 6
- out_grad: bfloat16 [4096, 7168], P('exp', 'seq'), may hold values from -6 to 6
- expert_ids: int32 [4096, 8], P('exp'), may hold values from 0 to 255, as said below
- route_weights: float32 [4096, 8], P('exp'), may hold values from 0.2 to 2.5
- gate_proj: bfloat16 [32, 7168, 2048], P('exp', None, 'seq'), may hold values from -0.0625 to 0.0625
- up_proj: bfloat16 [32, 7168, 2048], P('exp', None, 'seq'), may hold values from -0.0625 to 0.0625
- down_proj: bfloat16 [32, 2048, 7168], P('exp', 'seq'), may hold values from -0.125 to 0.125
Outputs:
- token_grad: bfloat16 [4096, 7168], P('exp', 'seq')
- route_grad: float32 [4096, 8], P('exp', 'seq')
Inputs may be any that keep to these rules, and one draw needn't show every extreme that they name: `expert_ids`: each row names 8 different experts, at most one of them below 32; between 96 and all of the 128 rows of one index of exp name one below 32; those rows name any one expert below 32 at most 8 times, and in every draw one such expert exactly 8 times on every index of exp.
All inputs are finite; a program needn't handle non-finite values.
Results may differ from a plain program's by a relative error of at most 0.0049.
Values may be sent and summed in bfloat16 or wider, within the bound.
A program may use at most 128 MiB of HBM per device.

v0:
```python
import jax
import jax.numpy as jnp
from jax import lax
from jax.sharding import PartitionSpec as P

PRECISE = lax.Precision.HIGHEST
CONTRACT = (((1,), (1,)), ((), ()))


def expert_front(row_inputs, row_grads, w_gate, w_up, w_down):
    pre_gate = jnp.dot(row_inputs, w_gate, preferred_element_type=jnp.float32)
    pre_up = jnp.dot(row_inputs, w_up, preferred_element_type=jnp.float32)
    back_grad = lax.dot_general(row_grads, w_down, CONTRACT, preferred_element_type=jnp.float32)
    gate_sig = jax.nn.sigmoid(pre_gate)
    active = pre_gate * gate_sig
    route_part = jnp.sum(active * pre_up * back_grad, axis=-1)
    grad_gate = (back_grad * pre_up * gate_sig * (1.0 + pre_gate * (1.0 - gate_sig))).astype(
        jnp.bfloat16
    )
    grad_up = (back_grad * active).astype(jnp.bfloat16)
    return (grad_gate, grad_up, route_part)


def expert_back(grad_gate, grad_up, w_gate, w_up):
    return lax.dot_general(
        grad_gate, w_gate, CONTRACT, preferred_element_type=jnp.float32
    ) + lax.dot_general(grad_up, w_up, CONTRACT, preferred_element_type=jnp.float32)


def slot_match(route_ids, most_rows, slot_count):
    expert_total = slot_count // most_rows
    named_hot = (route_ids[..., None] == jnp.arange(expert_total, dtype=jnp.int32)).astype(
        jnp.int32
    )
    per_token = jnp.sum(named_hot, axis=1)
    earlier = jnp.cumsum(per_token, axis=0) - per_token
    slot_rank = jnp.sum(named_hot * earlier[:, None, :], axis=-1)
    target = route_ids * most_rows + slot_rank
    return target[..., None] == jnp.arange(slot_count, dtype=jnp.int32)


def local(tokens, out_grad, expert_ids, route_weights, gate_proj, up_proj, down_proj):
    exp_count = lax.axis_size("exp")
    tok_dev = tokens.shape[0]
    expert_count = exp_count * gate_proj.shape[0]
    most_rows = max(2, 2 * ((tok_dev + expert_count - 1) // expert_count))
    slot_count = expert_count * most_rows
    w_gate = gate_proj[0]
    w_up = up_proj[0]
    w_down = down_proj[0]
    full_x, full_dy = (
        lax.all_gather(tokens, "seq", axis=1, tiled=True),
        lax.all_gather(out_grad, "seq", axis=1, tiled=True),
    )
    model_width = full_x.shape[1]
    matched = slot_match(expert_ids, most_rows, slot_count)
    selector = jnp.sum(matched, axis=1).astype(jnp.bfloat16)
    both_rows = jnp.concatenate([full_x, full_dy], axis=1)
    packed = jnp.einsum(
        "ts,td->sd", selector, both_rows, preferred_element_type=jnp.float32
    ).astype(jnp.bfloat16)
    packed = packed.reshape(expert_count, most_rows, 2 * model_width)
    weighted = jnp.sum(jnp.where(matched, route_weights[..., None], 0.0), axis=1)
    matched_float = matched.astype(jnp.float32)
    arrived = lax.all_to_all(packed, "exp", split_axis=0, concat_axis=0, tiled=True)
    layout = arrived.shape
    flat_rows = arrived.reshape(-1, layout[2])
    grad_gate, grad_up, route_part = expert_front(
        flat_rows[:, :model_width], flat_rows[:, model_width:], w_gate, w_up, w_down
    )
    slot_grad = expert_back(grad_gate, grad_up, w_gate, w_up).reshape(
        layout[0], layout[1], model_width
    )
    back_grad = lax.all_to_all(slot_grad, "exp", split_axis=0, concat_axis=0, tiled=True)
    back_route = lax.all_to_all(
        route_part.reshape(layout[0], layout[1]), "exp", split_axis=0, concat_axis=0, tiled=True
    )
    token_part = jnp.dot(weighted, back_grad.reshape(slot_count, model_width), precision=PRECISE)
    route_part = jnp.einsum(
        "tks,s->tk", matched_float, back_route.reshape(slot_count), precision=PRECISE
    )
    own_grad, own_route = (
        lax.psum_scatter(token_part, "seq", scatter_dimension=1, tiled=True),
        lax.psum_scatter(route_part, "seq", scatter_dimension=1, tiled=True),
    )
    return (own_grad.astype(jnp.bfloat16), own_route)


def solution(mesh):
    in_specs = (
        P("exp", "seq"),
        P("exp", "seq"),
        P("exp", None),
        P("exp", None),
        P("exp", None, "seq"),
        P("exp", None, "seq"),
        P("exp", "seq", None),
    )
    out_specs = (P("exp", "seq"), P("exp", "seq"))
    return jax.shard_map(local, mesh=mesh, in_specs=in_specs, out_specs=out_specs, check_vma=False)
```

profile of v0, /device:TPU:8, one launch (start us, length us, event | category | flops | bytes accessed | tf_op | source)
XLA Modules:
  0.0 482.7 jit_solution(10725312584192944092)
XLA Ops:
  7.2 0.0 all-gather.3.cloned.1.call-start
  7.2 0.7 all-gather.3.cloned.1.call-update
  7.9 0.0 all-gather.5.cloned.1.call-start
  7.9 0.7 all-gather.5.cloned.1.call-update
  8.6 0.7 convert_reduce_fusion.1
  9.4 0.1 copy.19
  9.5 0.2 reduce_window_sum.11
  9.6 0.1 copy.21
  9.7 0.7 select_reduce_fusion.1
  10.4 0.7 multiply_add_fusion
  11.1 0.1 copy.22
  11.2 0.4 convert_reduce_fusion
  11.6 28.5 %all-gather.3.cloned.1.call-done = bf16[128,7168]{1,0:T(8,128)(2,1)} async-done(((bf16[128,896]{1,0:T(8,128)(2,1)}), bf16[128,7168]{1,0:T(8,128)(2,1)}) %all-gather.3.cloned.1.call-update) | async-done | bytes 1835024 | tf_op jit(solution)/shard_map/all_gather | solution.py:52
  40.2 29.5 %all-gather.5.cloned.1.call-done = bf16[128,7168]{1,0:T(8,128)(2,1)} async-done(((bf16[128,896]{1,0:T(8,128)(2,1)}), bf16[128,7168]{1,0:T(8,128)(2,1)}) %all-gather.5.cloned.1.call-update) | async-done | bytes 1835024 | tf_op jit(solution)/shard_map/all_gather | solution.py:53
  69.7 4.1 fusion
  73.8 0.0 copy-start.1
  73.8 171.5 %all_to_all.19 = bf16[32,8,14336]{2,1,0:T(8,128)(2,1)S(1)} all-to-all(bf16[32,8,14336]{2,1,0:T(8,128)(2,1)S(1)} %fusion), channel_id=1, replica_groups=mesh['seq'=8,'exp'=32] {'exp'}, dimensions={0} | all-to-all | bytes 14680064 | tf_op jit(solution)/shard_map/all_to_all | solution.py:65
  245.4 0.0 copy-done.1
  245.4 0.0 copy-start
  245.4 1.6 fusion.11
  247.0 0.4 copy-done
  247.4 0.0 copy-start.3
  247.4 1.6 fusion.14
  249.0 0.4 copy-done.3
  249.5 1.2 multiply_reduce_fusion
  250.6 1.2 fusion.9
  251.9 4.2 fusion.1
  256.1 0.0 copy-start.2
  256.1 7.8 %all-to-all-start.1 = ((f32[32,8,7168]{2,1,0:T(8,128)}), f32[32,8,7168]{2,1,0:T(8,128)}, u32[]{:S(2)}, u32[]{:S(2)}) async-start(f32[32,8,7168]{2,1,0:T(8,128)} %fusion.1), calls=%async_computation.1 | async-start | bytes 14680064 | tf_op jit(solution)/shard_map/all_to_all | solution.py:74
  263.9 0.2 reduce-scatter.2.cloned.1.call-start
  264.1 0.0 copy-done.2
  264.2 0.1 copy.23
  264.3 0.4 select_reduce_fusion
  264.6 160.9 %all-to-all-done.1 = f32[32,8,7168]{2,1,0:T(8,128)} async-done(((f32[32,8,7168]{2,1,0:T(8,128)}), f32[32,8,7168]{2,1,0:T(8,128)}, u32[]{:S(2)}, u32[]{:S(2)}) %all-to-all-start.1) | async-done | bytes 7340064 | tf_op jit(solution)/shard_map/all_to_all | solution.py:74
  425.5 9.1 %fusion.2 = f32[128,7168]{1,0:T(8,128)} fusion(f32[128,256]{1,0:T(8,128)S(1)} %select_reduce_fusion, f32[32,8,7168]{2,1,0:T(8,128)} %all-to-all-done.1), kind=kOutput, calls=%fused_computation.4 | convolution fusion | flops 2818572288 | bytes 11141120 | tf_op jit(solution)/shard_map/dot_general | solution.py:78
  434.6 0.0 copy-start.4
  434.6 0.0 reduce-scatter.2.cloned.1.call-update
  434.7 0.7 all_to_all.14
  435.4 9.9 %all-to-all-start.2 = ((f32[32,1,8]{2,1,0:T(1,128)}), f32[32,1,8]{2,1,0:T(1,128)S(1)}, u32[]{:S(2)}, u32[]{:S(2)}) async-start(f32[32,1,8]{2,1,0:T(1,128)} %bitcast.7), calls=%async_computation.3 | async-start | bytes 32768 | tf_op jit(solution)/shard_map/all_to_all | solution.py:75
  445.3 0.0 copy-done.4
  445.3 0.6 dynamic-slice
  445.9 7.9 %all-to-all-done.2 = f32[32,1,8]{2,1,0:T(1,128)S(1)} async-done(((f32[32,1,8]{2,1,0:T(1,128)}), f32[32,1,8]{2,1,0:T(1,128)S(1)}, u32[]{:S(2)}, u32[]{:S(2)}) %all-to-all-start.2) | async-done | bytes 1056 | tf_op jit(solution)/shard_map/all_to_all | solution.py:75
  453.8 0.5 broadcast.25
  454.3 0.7 reduce.3
  455.0 0.1 reshape.41
  455.1 3.6 fusion.19
  458.8 0.1 copy.25
  458.8 12.5 %all-reduce = f32[128,8]{0,1:T(8,128)S(1)} all-reduce(f32[128,8]{0,1:T(8,128)S(1)} %bitcast.31), channel_id=3, replica_groups=mesh['seq'=8,'exp'=32] {'seq'}, use_global_device_ids=true, to_apply=%region_7.8.clone | all-reduce | flops 1024 | bytes 8192
  471.4 1.2 constant_dynamic-slice_fusion
  472.5 1.9 reduce-scatter.2.cloned.1.call-done
  474.4 1.7 convert_element_type.28
  (1 shorter events, 0.0 us)
Async XLA Ops:
  7.2 33.0 %all-gather.3.cloned.1.call-start = ((), (), s32[]{:S(2)}) async-start(), calls=%async_computation.4 | async-start | bytes 2064384 | tf_op jit(solution)/shard_map/all_gather | solution.py:52
  7.9 61.8 %all-gather.5.cloned.1.call-start = ((), (), s32[]{:S(2)}) async-start(), calls=%async_computation.5 | async-start | bytes 2064384 | tf_op jit(solution)/shard_map/all_gather | solution.py:53
  73.8 171.5 %copy-start.1 = (bf16[1,7168,256]{2,1,0:T(8,128)(2,1)S(1)}, bf16[1,7168,256]{2,1,0:T(8,128)(2,1)}, u32[]{:S(2)}) copy-start(bf16[1,7168,256]{2,1,0:T(8,128)(2,1)} %param.11) | copy-start | bytes 11010052
  245.4 2.0 copy-start
  247.4 2.0 copy-start.3
  256.1 8.0 %copy-start.2 = (f32[128,8]{0,1:T(8,128)S(1)}, f32[128,8]{0,1:T(8,128)}, u32[]{:S(2)}) copy-start(f32[128,8]{0,1:T(8,128)} %param.10) | copy-start | bytes 12292
  256.1 169.4 %all-to-all-start.1 = ((f32[32,8,7168]{2,1,0:T(8,128)}), f32[32,8,7168]{2,1,0:T(8,128)}, u32[]{:S(2)}, u32[]{:S(2)}) async-start(f32[32,8,7168]{2,1,0:T(8,128)} %fusion.1), calls=%async_computation.1 | async-start | bytes 14680064 | tf_op jit(solution)/shard_map/all_to_all | solution.py:74
  263.9 210.5 %reduce-scatter.2.cloned.1.call-start = ((), (), s32[]{:S(2)}) async-start(), calls=%async_computation.6 | async-start | bytes 4128768 | tf_op jit(solution)/shard_map/reduce_scatter | solution.py:83
  434.6 10.6 %copy-start.4 = (u32[256]{0:T(256)S(1)}, u32[256]{0:T(256)}, u32[]{:S(2)}) copy-start(u32[256]{0:T(256)} %constant.17) | copy-start | bytes 3076
  435.4 18.5 %all-to-all-start.2 = ((f32[32,1,8]{2,1,0:T(1,128)}), f32[32,1,8]{2,1,0:T(1,128)S(1)}, u32[]{:S(2)}, u32[]{:S(2)}) async-start(f32[32,1,8]{2,1,0:T(1,128)} %bitcast.7), calls=%async_computation.3 | async-start | bytes 32768 | tf_op jit(solution)/shard_map/all_to_all | solution.py:75
Sparse Core Ops, SparseCore 0:
  9.8 30.2 all-gather.2
  42.0 27.6 all-gather.4
  434.8 39.5 reduce-scatter.1
where the time goes:
time: 483 us
  waiting for transfers between devices  230 us (48%)
  blocking collectives  184 us (38%)
  matrix products  26.7 us (6%)
  starting transfers between devices  18 us (4%)
  between operations  13.9 us (3%)
  other arithmetic  5.49 us (1%)
    all_to_all x1, blocking collectives, local(): lax.all_to_all(packed, 'exp', split_axis=0, concat_axis=0, tiled=True)  172 us
    all_to_all x1, waiting for transfers between devices, local(): lax.all_to_all(slot_grad, 'exp', split_axis=0, concat_axis=0, tiled=True)  161 us
    all_gather x1, waiting for transfers between devices, local(): lax.all_gather(out_grad, 'seq', axis=1, tiled=True)  29.5 us
    all_gather x1, waiting for transfers between devices, local(): lax.all_gather(tokens, 'seq', axis=1, tiled=True)  28.5 us
    unnamed x1, blocking collectives  12.5 us
    all_to_all x1, starting transfers between devices, local(): lax.all_to_all(route_part.reshape(layout[0], layout[1]), 'exp', split_axi...  9.9 us
  transfers between devices with their start and end apart: 5, of which 5 were waited for; matrix products, arithmetic and copies ran while one was open for 2% of the time, Pallas kernels for 0%

commit v1 on v0

--- a/solution.py
+++ b/solution.py
@@ -5,6 +5,13 @@
 
 PRECISE = lax.Precision.HIGHEST
 CONTRACT = (((1,), (1,)), ((), ()))
+
+
+def exchange_gather(array, name, along):
+    size = lax.axis_size(name)
+    shards = jnp.stack([array for _ in range(size)])
+    shards = lax.all_to_all(shards, name, split_axis=0, concat_axis=0)
+    return jnp.concatenate(shards, axis=along)
 
 
 def expert_front(row_inputs, row_grads, w_gate, w_up, w_down):
@@ -50,7 +57,7 @@
     w_down = down_proj[0]
     full_x, full_dy = (
         lax.all_gather(tokens, "seq", axis=1, tiled=True),
-        lax.all_gather(out_grad, "seq", axis=1, tiled=True),
+        exchange_gather(out_grad, "seq", 1),
     )
     model_width = full_x.shape[1]
     matched = slot_match(expert_ids, most_rows, slot_count)

time: 483 us -> 464 us (0.961)
  waiting for transfers between devices: 230 us -> 200 us
  local copies, waits for them, and re-layouts: 4.42 us -> 11 us
    all_to_all x0 -> x1, waiting for transfers between devices: none -> 30.8 us  [exchange_gather(): shards = lax.all_to_all(shards, name, split_axis=0, concat_axis=0)]
    all_gather x1 -> x0, waiting for transfers between devices: 29.5 us -> none  [local(): lax.all_gather(out_grad, 'seq', axis=1, tiled=True)]
    all_gather x1, waiting for transfers between devices: 28.5 us -> 0.01 us  [local(): lax.all_gather(tokens, 'seq', axis=1, tiled=True)]
  transfers between devices with their start and end apart: 5 -> 5, of which waited for: 5 -> 4; matrix products, arithmetic and copies ran while one was open for 2% -> 3% of each run, Pallas kernels for 0% -> 0%
where the time goes in v1:
time: 464 us; the launch traced here: 463 us
  waiting for transfers between devices  200 us (43%)
  blocking collectives  185 us (40%)
  matrix products  26.7 us (6%)
  starting transfers between devices  22.5 us (5%)
  between operations  14.2 us (3%)
  local copies, waits for them, and re-layouts  11 us (2%)
    all_to_all x1, blocking collectives, local(): lax.all_to_all(packed, 'exp', split_axis=0, concat_axis=0, tiled=True)  173 us
    all_to_all x1, waiting for transfers between devices, local(): lax.all_to_all(slot_grad, 'exp', split_axis=0, concat_axis=0, tiled=True)  160 us
    all_to_all x1, waiting for transfers between devices, exchange_gather(): shards = lax.all_to_all(shards, name, split_axis=0, concat_axis=0)  30.8 us
    unnamed x1, blocking collectives  12.7 us
    all_to_all x1, starting transfers between devices, local(): lax.all_to_all(route_part.reshape(layout[0], layout[1]), 'exp', split_axi...  10.4 us
  transfers between devices with their start and end apart: 5, of which 4 were waited for; matrix products, arithmetic and copies ran while one was open for 3% of the time, Pallas kernels for 0%

profile of v1, /device:TPU:8, one launch (start us, length us, event | category | flops | bytes accessed | tf_op | source)
XLA Modules:
  0.0 463.4 jit_solution(879313617349607932)
XLA Ops:
  7.2 0.0 copy-start.2
  7.2 0.0 all-gather.2.cloned.1.call-start
  7.2 1.8 copy.30
  9.0 0.0 all-gather.2.cloned.1.call-update
  9.0 2.4 stack.2
  11.4 4.3 all-to-all-start
  15.7 0.0 copy-done.2
  15.7 0.1 copy.25
  15.8 0.2 reduce_window_sum.11
  16.0 0.1 copy.27
  16.1 0.1 copy.28
  16.3 0.4 convert_reduce_fusion
  16.6 30.8 %all-to-all-done = bf16[8,128,896]{2,1,0:T(8,128)(2,1)S(1)} async-done(((bf16[8,128,896]{2,1,0:T(8,128)(2,1)}), bf16[8,128,896]{2,1,0:T(8,128)(2,1)S(1)}, u32[]{:S(2)}, u32[]{:S(2)}) %all-to-all-start) | async-done | bytes 1835040 | tf_op jit(solution)/shard_map/all_to_all | solution.py:13
  47.4 2.4 copy.31
  49.8 0.0 all-gather.2.cloned.1.call-done
  49.8 4.1 fusion
  54.0 0.0 copy-start.1
  54.0 172.7 %all_to_all.24 = bf16[32,8,14336]{2,1,0:T(8,128)(2,1)S(1)} all-to-all(bf16[32,8,14336]{2,1,0:T(8,128)(2,1)S(1)} %fusion), channel_id=1, replica_groups=mesh['seq'=8,'exp'=32] {'exp'}, dimensions={0} | all-to-all | bytes 14680064 | tf_op jit(solution)/shard_map/all_to_all | solution.py:72
  226.7 0.0 copy-done.1
  226.7 0.0 copy-start
  226.7 1.6 fusion.11
  228.3 0.4 copy-done
  228.7 0.0 copy-start.4
  228.8 1.6 fusion.14
  230.4 0.4 copy-done.4
  230.8 1.2 multiply_reduce_fusion
  232.0 1.2 fusion.9
  233.2 4.2 fusion.1
  237.4 0.0 copy-start.3
  237.4 7.5 %all-to-all-start.2 = ((f32[32,8,7168]{2,1,0:T(8,128)}), f32[32,8,7168]{2,1,0:T(8,128)}, u32[]{:S(2)}, u32[]{:S(2)}) async-start(f32[32,8,7168]{2,1,0:T(8,128)} %fusion.1), calls=%async_computation.2 | async-start | bytes 14680064 | tf_op jit(solution)/shard_map/all_to_all | solution.py:81
  244.9 0.2 reduce-scatter.2.cloned.1.call-start
  245.1 0.0 copy-done.3
  245.2 0.1 copy.29
  245.3 0.4 select_reduce_fusion
  245.6 160.4 %all-to-all-done.2 = f32[32,8,7168]{2,1,0:T(8,128)} async-done(((f32[32,8,7168]{2,1,0:T(8,128)}), f32[32,8,7168]{2,1,0:T(8,128)}, u32[]{:S(2)}, u32[]{:S(2)}) %all-to-all-start.2) | async-done | bytes 7340064 | tf_op jit(solution)/shard_map/all_to_all | solution.py:81
  406.0 9.1 %fusion.2 = f32[128,7168]{1,0:T(8,128)} fusion(f32[128,256]{1,0:T(8,128)S(1)} %select_reduce_fusion, f32[32,8,7168]{2,1,0:T(8,128)} %all-to-all-done.2), kind=kOutput, calls=%fused_computation.4 | convolution fusion | flops 2818572288 | bytes 11141120 | tf_op jit(solution)/shard_map/dot_general | solution.py:85
  415.2 0.0 copy-start.5
  415.2 0.0 reduce-scatter.2.cloned.1.call-update
  415.2 0.7 all_to_all.18
  415.9 10.4 %all-to-all-start.3 = ((f32[32,1,8]{2,1,0:T(1,128)}), f32[32,1,8]{2,1,0:T(1,128)S(1)}, u32[]{:S(2)}, u32[]{:S(2)}) async-start(f32[32,1,8]{2,1,0:T(1,128)} %bitcast.9), calls=%async_computation.4 | async-start | bytes 32768 | tf_op jit(solution)/shard_map/all_to_all | solution.py:82
  426.3 0.0 copy-done.5
  426.3 0.6 dynamic-slice
  427.0 7.9 %all-to-all-done.3 = f32[32,1,8]{2,1,0:T(1,128)S(1)} async-done(((f32[32,1,8]{2,1,0:T(1,128)}), f32[32,1,8]{2,1,0:T(1,128)S(1)}, u32[]{:S(2)}, u32[]{:S(2)}) %all-to-all-start.3) | async-done | bytes 1056 | tf_op jit(solution)/shard_map/all_to_all | solution.py:82
  434.9 0.5 broadcast.27
  435.4 0.7 reduce.3
  436.1 0.1 reshape.51
  436.2 3.6 fusion.19
  439.8 0.1 copy.33
  439.9 12.7 %all-reduce = f32[128,8]{0,1:T(8,128)S(1)} all-reduce(f32[128,8]{0,1:T(8,128)S(1)} %bitcast.35), channel_id=3, replica_groups=mesh['seq'=8,'exp'=32] {'seq'}, use_global_device_ids=true, to_apply=%region_7.8.clone | all-reduce | flops 1024 | bytes 8192
  452.5 1.2 constant_dynamic-slice_fusion
  453.7 1.2 reduce-scatter.2.cloned.1.call-done
  454.9 1.7 convert_element_type.28
  (4 shorter events, 0.1 us)
Async XLA Ops:
  7.2 8.6 %copy-start.2 = (s32[128,8]{0,1:T(8,128)S(1)}, s32[128,8]{0,1:T(8,128)}, u32[]{:S(2)}) copy-start(s32[128,8]{0,1:T(8,128)} %param.9) | copy-start | bytes 12292
  7.2 42.7 %all-gather.2.cloned.1.call-start = ((), (), s32[]{:S(2)}) async-start(), calls=%async_computation.5 | async-start | bytes 2064384 | tf_op jit(solution)/shard_map/all_gather | solution.py:59
  11.4 36.0 %all-to-all-start = ((bf16[8,128,896]{2,1,0:T(8,128)(2,1)}), bf16[8,128,896]{2,1,0:T(8,128)(2,1)S(1)}, u32[]{:S(2)}, u32[]{:S(2)}) async-start(bf16[8,128,896]{2,1,0:T(8,128)(2,1)} %stack.2), calls=%async_computation | async-start | bytes 3670016 | tf_op jit(solution)/shard_map/all_to_all | solution.py:13
  54.0 172.7 %copy-start.1 = (bf16[1,7168,256]{2,1,0:T(8,128)(2,1)S(1)}, bf16[1,7168,256]{2,1,0:T(8,128)(2,1)}, u32[]{:S(2)}) copy-start(bf16[1,7168,256]{2,1,0:T(8,128)(2,1)} %param.11) | copy-start | bytes 11010052
  226.7 2.0 copy-start
  228.7 2.0 copy-start.4
  237.4 7.7 %copy-start.3 = (f32[128,8]{0,1:T(8,128)S(1)}, f32[128,8]{0,1:T(8,128)}, u32[]{:S(2)}) copy-start(f32[128,8]{0,1:T(8,128)} %param.10) | copy-start | bytes 12292
  237.4 168.6 %all-to-all-start.2 = ((f32[32,8,7168]{2,1,0:T(8,128)}), f32[32,8,7168]{2,1,0:T(8,128)}, u32[]{:S(2)}, u32[]{:S(2)}) async-start(f32[32,8,7168]{2,1,0:T(8,128)} %fusion.1), calls=%async_computation.2 | async-start | bytes 14680064 | tf_op jit(solution)/shard_map/all_to_all | solution.py:81
  244.9 210.0 %reduce-scatter.2.cloned.1.call-start = ((), (), s32[]{:S(2)}) async-start(), calls=%async_computation.6 | async-start | bytes 4128768 | tf_op jit(solution)/shard_map/reduce_scatter | solution.py:90
  415.2 11.2 %copy-start.5 = (u32[256]{0:T(256)S(1)}, u32[256]{0:T(256)}, u32[]{:S(2)}) copy-start(u32[256]{0:T(256)} %constant.17) | copy-start | bytes 3076
  415.9 19.0 %all-to-all-start.3 = ((f32[32,1,8]{2,1,0:T(1,128)}), f32[32,1,8]{2,1,0:T(1,128)S(1)}, u32[]{:S(2)}, u32[]{:S(2)}) async-start(f32[32,1,8]{2,1,0:T(1,128)} %bitcast.9), calls=%async_computation.4 | async-start | bytes 32768 | tf_op jit(solution)/shard_map/all_to_all | solution.py:82
Sparse Core Ops, SparseCore 0:
  10.4 34.8 all-gather.1
  415.3 39.5 reduce-scatter.1
